TPU v7x, 32 devices: a whole 2x2x4 slice. The times are simulated.
32 devices in a mesh: trip: 4 (over x, core), exc: 8 (over z, y).
Axes of the slice: x: 2, y: 2, z: 4, core: 2. Of those that a mesh axis runs over, the one named last changes fastest.
Arguments:
- pes_grids: float32 [128, 16, 256], P(('trip', 'exc')), may hold values from -6 to 6
- modals: float32 [200, 128], P('trip'), may hold values from -1.8 to 1.8
- energies: float32 [200, 8], P('trip'), may hold values from 0.05 to 0.5
- triple_modes: int32 [128, 3], P(('trip', 'exc')), may hold values from 0 to 199, as said below
- routing: int32 [4, 8, 8], P('trip', None, 'exc'), may hold values from 0 to 3
- block_source: int32 [768], P(('trip', 'exc')), may hold values from 0 to 7
- live_rows: int32 [768], P(('trip', 'exc')), may hold values from 1 to 8
- trial_vectors: bfloat16 [768, 512, 512], P(('trip', 'exc')), may hold values from -6 to 6
- spectator_energy: float32 [768, 8], P(('trip', 'exc')), may hold values from 0.1 to 1
Outputs:
- sigma_blocks: bfloat16 [768, 512, 512], P(('trip', 'exc'))
Inputs may be any that keep to these rules, and one draw needn't show every extreme that they name: `triple_modes`: the three modes of a triple are distinct.
All inputs are finite; a program needn't handle non-finite values.
Results may differ from a plain program's by a relative error of at most 0.005.
Values may be sent and summed in bfloat16 or wider, within the bound.
A program may use at most 128 MiB of HBM per device.

v0:
```python
import jax
import jax.numpy as jnp
from jax import lax
from jax.sharding import PartitionSpec as P

NMOD = 8
G = 16
NVEC = 64
ROWS = 8


def integrals(grid_values, modal_rows, level_rows):
    shaped = modal_rows.reshape(3, NMOD, G)
    paired = (shaped[:, :, None, :] * shaped[:, None, :, :]).reshape(3, NMOD * NMOD, G)
    grid_cube = grid_values.reshape(G, G, G)
    section_one = jnp.einsum("xyz,cz->xyc", grid_cube, paired[2], precision=lax.Precision.HIGHEST)
    section_two = jnp.einsum("xyc,by->xbc", section_one, paired[1], precision=lax.Precision.HIGHEST)
    tensor = jnp.einsum("xbc,ax->abc", section_two, paired[0], precision=lax.Precision.HIGHEST)
    states = NMOD * NMOD * NMOD
    matrix = (
        tensor.reshape(NMOD, NMOD, NMOD, NMOD, NMOD, NMOD)
        .transpose(0, 2, 4, 1, 3, 5)
        .reshape(states, states)
    )
    diagonal = (
        level_rows[0][:, None, None] + level_rows[1][None, :, None] + level_rows[2][None, None, :]
    ).reshape(states)
    return (matrix + jnp.diag(diagonal)).astype(jnp.bfloat16)


def apply_block(matrix, coeff_block, spec_row, live_count):
    product = jnp.dot(matrix, coeff_block, preferred_element_type=jnp.float32)
    spread = jnp.repeat(spec_row, NVEC)
    summed = product + spread[None, :] * coeff_block.astype(jnp.float32)
    column_rows = jnp.arange(ROWS * NVEC, dtype=jnp.int32) // NVEC
    return jnp.where((column_rows < live_count)[None, :], summed, 0.0).astype(jnp.bfloat16)


def transform_packed(packed):
    return integrals(packed[0], packed[1], packed[2])


def on_device(
    pes_grids,
    modals,
    energies,
    triple_modes,
    routing,
    block_source,
    live_rows,
    trial_vectors,
    spectator_energy,
):
    tables, levels = (
        lax.all_gather(modals, "trip", axis=0, tiled=True),
        lax.all_gather(energies, "trip", axis=0, tiled=True),
    )
    flat_modes = triple_modes.reshape(-1)
    onehot = (flat_modes[:, None] == jnp.arange(tables.shape[0], dtype=jnp.int32)[None, :]).astype(
        jnp.float32
    )
    modal_rows = jnp.dot(onehot, tables, precision=lax.Precision.HIGHEST).reshape(
        -1, 3, tables.shape[1]
    )
    level_rows = jnp.dot(onehot, levels, precision=lax.Precision.HIGHEST).reshape(
        -1, 3, levels.shape[1]
    )
    targets = routing[0, :, 0]
    owned = lax.map(transform_packed, (pes_grids, modal_rows, level_rows))
    received = lax.all_to_all(
        jnp.take(owned, targets, axis=0), "exc", split_axis=0, concat_axis=0, tiled=True
    )

    def one_block(packed):
        source, coeff_block, spec_row, live_count = packed
        matrix = lax.dynamic_index_in_dim(received, source, 0, keepdims=False)
        return apply_block(matrix, coeff_block, spec_row, live_count)

    return lax.map(one_block, (block_source, trial_vectors, spectator_energy, live_rows))


def solution(mesh):
    in_specs = (
        P(("trip", "exc"), None, None),
        P("trip", None),
        P("trip", None),
        P(("trip", "exc"), None),
        P("trip", None, "exc"),
        P(("trip", "exc")),
        P(("trip", "exc")),
        P(("trip", "exc"), None, None),
        P(("trip", "exc"), None),
    )
    out_specs = P(("trip", "exc"), None, None)
    return jax.shard_map(
        on_device, mesh=mesh, in_specs=in_specs, out_specs=out_specs, check_vma=False
    )
```

profile of v0, /device:TPU:0, one launch (start us, length us, event | category | flops | bytes accessed | tf_op | source)
XLA Modules:
  0.0 551.2 jit_solution(16131159881954322903)
XLA Ops:
  2.1 6.6 %all-gather = f32[4,50,128]{2,1,0:T(8,128)S(1)} all-gather(f32[1,50,128]{2,1,0:T(8,128)} %bitcast.94), channel_id=1, replica_groups=mesh['trip'=4,'exc'=8] {'trip'}, dimensions={0}, use_global_device_ids=true | all-gather | bytes 128000 | tf_op jit(solution)/shard_map/all_gather | solution.py:55
  8.9 5.6 %all-gather.1 = f32[4,50,8]{1,2,0:T(8,128)S(1)} all-gather(f32[1,50,8]{1,2,0:T(8,128)} %bitcast.95), channel_id=1, replica_groups=mesh['trip'=4,'exc'=8] {'trip'}, dimensions={0}, use_global_device_ids=true | all-gather | bytes 8000 | tf_op jit(solution)/shard_map/all_gather | solution.py:56
  14.8 272.2 %while.22 = (s32[]{:T(128)}, bf16[4,512,512]{2,1,0:T(8,128)(2,1)}, f32[4,3,128]{2,1,0:T(4,128)S(1)}, f32[4,16,256]{2,1,0:T(8,128)}, f32[4,3,8]{2,1,0:T(4,128)S(1)}, /*index=5*/s32[]{:T(128)}) while((s32[]{:T(128)}, bf16[4,512,512]{2,1,0:T(8,128)(2,1)}, f32[4,3,128]{2,1,0:T(4,128)S(1)}, f32[4,16,256]{2,1,0:T(8,128)}, f32[4,3,8]{2,1,0:T(4,128)S(1)}, ...), condition=%wide.region_1.2_spmd, body=%wide.region_0.1_spmd.sunk | while | flops 67112512 | bytes 10220593 | solution.py:69
  17.2 36.6 %convolution_bitcast_fusion.5 = f32[8,8,8,8,8,8]{5,3,2,4,1,0:T(8,128)S(1)} fusion(f32[8,8,8,8,16,1]{4,3,2,1,0,5:T(8,128)S(1)} %bitcast.93, f32[3,8,8,16]{3,2,1,0:T(8,128)S(1)} %broadcast_multiply_fusion.2), kind=kOutput, calls=%fused_computation.1.clone.1 | convolution fusion | flops 50331648 | bytes 3178496 | tf_op jit(solution)/shard_map/while/body/eval_jaxpr/xbc,ax->abc/dot_general | solution.py:18
  53.8 15.2 %copy.43 = f32[8,8,8,8,8,8]{5,4,3,2,1,0:T(8,128)} copy(f32[8,8,8,8,8,8]{5,3,2,4,1,0:T(8,128)S(1)} %convolution_bitcast_fusion.5) | data formatting | bytes 2097152 | tf_op jit(solution)/shard_map/while/body/eval_jaxpr/transpose | solution.py:22
  69.0 12.6 %reshape.208 = f32[1,512,512]{2,1,0:T(8,128)S(1)} reshape(f32[8,8,8,8,8,8]{5,4,3,2,1,0:T(8,128)} %copy.43) | data formatting | bytes 2097152 | tf_op jit(solution)/shard_map/while/body/eval_jaxpr/reshape | solution.py:23
  85.3 36.6 %convolution_bitcast_fusion.5 = f32[8,8,8,8,8,8]{5,3,2,4,1,0:T(8,128)S(1)} fusion(f32[8,8,8,8,16,1]{4,3,2,1,0,5:T(8,128)S(1)} %bitcast.93, f32[3,8,8,16]{3,2,1,0:T(8,128)S(1)} %broadcast_multiply_fusion.2), kind=kOutput, calls=%fused_computation.1.clone.1 | convolution fusion | flops 50331648 | bytes 3178496 | tf_op jit(solution)/shard_map/while/body/eval_jaxpr/xbc,ax->abc/dot_general | solution.py:18
  121.9 15.2 %copy.43 = f32[8,8,8,8,8,8]{5,4,3,2,1,0:T(8,128)} copy(f32[8,8,8,8,8,8]{5,3,2,4,1,0:T(8,128)S(1)} %convolution_bitcast_fusion.5) | data formatting | bytes 2097152 | tf_op jit(solution)/shard_map/while/body/eval_jaxpr/transpose | solution.py:22
  137.1 12.6 %reshape.208 = f32[1,512,512]{2,1,0:T(8,128)S(1)} reshape(f32[8,8,8,8,8,8]{5,4,3,2,1,0:T(8,128)} %copy.43) | data formatting | bytes 2097152 | tf_op jit(solution)/shard_map/while/body/eval_jaxpr/reshape | solution.py:23
  153.3 36.6 %convolution_bitcast_fusion.5 = f32[8,8,8,8,8,8]{5,3,2,4,1,0:T(8,128)S(1)} fusion(f32[8,8,8,8,16,1]{4,3,2,1,0,5:T(8,128)S(1)} %bitcast.93, f32[3,8,8,16]{3,2,1,0:T(8,128)S(1)} %broadcast_multiply_fusion.2), kind=kOutput, calls=%fused_computation.1.clone.1 | convolution fusion | flops 50331648 | bytes 3178496 | tf_op jit(solution)/shard_map/while/body/eval_jaxpr/xbc,ax->abc/dot_general | solution.py:18
  189.9 15.2 %copy.43 = f32[8,8,8,8,8,8]{5,4,3,2,1,0:T(8,128)} copy(f32[8,8,8,8,8,8]{5,3,2,4,1,0:T(8,128)S(1)} %convolution_bitcast_fusion.5) | data formatting | bytes 2097152 | tf_op jit(solution)/shard_map/while/body/eval_jaxpr/transpose | solution.py:22
  205.1 12.6 %reshape.208 = f32[1,512,512]{2,1,0:T(8,128)S(1)} reshape(f32[8,8,8,8,8,8]{5,4,3,2,1,0:T(8,128)} %copy.43) | data formatting | bytes 2097152 | tf_op jit(solution)/shard_map/while/body/eval_jaxpr/reshape | solution.py:23
  221.4 36.6 %convolution_bitcast_fusion.5 = f32[8,8,8,8,8,8]{5,3,2,4,1,0:T(8,128)S(1)} fusion(f32[8,8,8,8,16,1]{4,3,2,1,0,5:T(8,128)S(1)} %bitcast.93, f32[3,8,8,16]{3,2,1,0:T(8,128)S(1)} %broadcast_multiply_fusion.2), kind=kOutput, calls=%fused_computation.1.clone.1 | convolution fusion | flops 50331648 | bytes 3178496 | tf_op jit(solution)/shard_map/while/body/eval_jaxpr/xbc,ax->abc/dot_general | solution.py:18
  258.0 15.2 %copy.43 = f32[8,8,8,8,8,8]{5,4,3,2,1,0:T(8,128)} copy(f32[8,8,8,8,8,8]{5,3,2,4,1,0:T(8,128)S(1)} %convolution_bitcast_fusion.5) | data formatting | bytes 2097152 | tf_op jit(solution)/shard_map/while/body/eval_jaxpr/transpose | solution.py:22
  273.2 12.6 %reshape.208 = f32[1,512,512]{2,1,0:T(8,128)S(1)} reshape(f32[8,8,8,8,8,8]{5,4,3,2,1,0:T(8,128)} %copy.43) | data formatting | bytes 2097152 | tf_op jit(solution)/shard_map/while/body/eval_jaxpr/reshape | solution.py:23
  287.0 4.4 gather_fusion
  291.4 4.6 broadcast_select_fusion
  296.1 6.2 %all-to-all-start = ((bf16[8,512,512]{2,1,0:T(8,128)(2,1)}), bf16[8,512,512]{2,1,0:T(8,128)(2,1)}, u32[]{:S(2)}, u32[]{:S(2)}) async-start(bf16[8,512,512]{2,1,0:T(8,128)(2,1)} %broadcast_select_fusion), calls=%async_computation | async-start | bytes 8388608 | tf_op jit(solution)/shard_map/all_to_all | solution.py:70
  302.3 93.7 %all-to-all-done = bf16[8,512,512]{2,1,0:T(8,128)(2,1)} async-done(((bf16[8,512,512]{2,1,0:T(8,128)(2,1)}), bf16[8,512,512]{2,1,0:T(8,128)(2,1)}, u32[]{:S(2)}, u32[]{:S(2)}) %all-to-all-start) | async-done | bytes 4194336 | tf_op jit(solution)/shard_map/all_to_all | solution.py:70
  396.1 155.1 %while.23 = (s32[]{:T(128)}, bf16[24,512,512]{2,1,0:T(8,128)(2,1)}, s32[24]{0:T(128)S(1)}, s32[24]{0:T(128)S(1)}, bf16[8,512,512]{2,1,0:T(8,128)(2,1)}, /*index=...) while((s32[]{:T(128)}, bf16[24,512,512]{2,1,0:T(8,128)(2,1)}, ...), condition=%wide.region_3.4_spmd, body=%wide.region_2.3_spmd.sunk | while | flops 269750784 | bytes 2107659 | solution.py:79
  406.3 2.7 fusion.45
  425.7 2.7 fusion.45
  438.7 2.7 fusion.45
  477.5 2.7 fusion.45
  (240 shorter events, 117.1 us)
Async XLA Ops:
  296.1 6.2 %copy-start = (f32[24,8]{0,1:T(8,128)S(1)}, f32[24,8]{0,1:T(8,128)}, u32[]{:S(2)}) copy-start(f32[24,8]{0,1:T(8,128)} %param.21) | copy-start | bytes 2308
  296.1 100.0 %copy-start.1 = (s32[24]{0:T(128)S(1)}, s32[24]{0:T(128)}, u32[]{:S(2)}) copy-start(s32[24]{0:T(128)} %param.19) | copy-start | bytes 292
  296.1 100.0 %copy-start.2 = (s32[24]{0:T(128)S(1)}, s32[24]{0:T(128)}, u32[]{:S(2)}) copy-start(s32[24]{0:T(128)} %param.18) | copy-start | bytes 292
  296.1 100.0 %all-to-all-start = ((bf16[8,512,512]{2,1,0:T(8,128)(2,1)}), bf16[8,512,512]{2,1,0:T(8,128)(2,1)}, u32[]{:S(2)}, u32[]{:S(2)}) async-start(bf16[8,512,512]{2,1,0:T(8,128)(2,1)} %broadcast_select_fusion), calls=%async_computation | async-start | bytes 8388608 | tf_op jit(solution)/shard_map/all_to_all | solution.py:70
where the time goes:
time: 554 us; the launch traced here: 551 us
  matrix products  213 us (38%)
  local copies, waits for them, and re-layouts  157 us (28%)
  waiting for transfers between devices  93.7 us (17%)
  loops' own time  44.5 us (8%)
  other arithmetic  25.1 us (5%)
  blocking collectives  12.2 us (2%)
  starting transfers between devices  6.19 us (1%)
    dot_general x4, matrix products, integrals(): jnp.einsum('xbc,ax->abc', section_two, paired[0], precision=lax.Precision...  146 us
    all_to_all x1, waiting for transfers between devices, on_device(): lax.all_to_all(jnp.take(owned, targets, axis=0), 'exc', split_axis=0, con...  93.7 us
    dot_general x24, matrix products, apply_block(): product = jnp.dot(matrix, coeff_block, preferred_element_type=jnp.float32)  62.9 us
    transpose x4, local copies, waits for them, and re-layouts, integrals(): matrix = tensor.reshape(NMOD, NMOD, NMOD, NMOD, NMOD, NMOD).transpose(0,...  60.9 us
    reshape x4, local copies, waits for them, and re-layouts, integrals(): matrix = tensor.reshape(NMOD, NMOD, NMOD, NMOD, NMOD, NMOD).transpose(0,...  50.4 us
    another operation x1, loops' own time, on_device(): lax.map(one_block, (block_source, trial_vectors, spectator_energy, live_r...  44.2 us
    dynamic_slice x48, local copies, waits for them, and re-layouts, on_device(): lax.map(one_block, (block_source, trial_vectors, spectator_energy, live_r...  29.4 us
    lt x24, other arithmetic, apply_block(): column_rows < live_count  14.7 us
  transfers between devices with their start and end apart: 1, of which 1 were waited for; matrix products, arithmetic and copies ran while one was open for 0% of the time, Pallas kernels for 0%

commit v1 on v0

v1 whole, which is shorter than its diff:
```python
import functools

import jax
import jax.numpy as jnp
from jax import lax
from jax.experimental import pallas as pl
from jax.experimental.pallas import tpu as pltpu
from jax.sharding import PartitionSpec as P

NMOD = 8
G = 16
F32 = jnp.float32
BF16 = jnp.bfloat16
MESH = pl.DeviceIdType.MESH
LANES = 128


def exchange(
    n_trip,
    n_exc,
    routing_ref,
    modes_ref,
    grids_ref,
    modals_ref,
    energies_ref,
    table_ref,
    levels_ref,
    grid_out_ref,
    mode_out_ref,
    send_grid,
    send_mode,
    trip_send,
    trip_recv,
    exc_send,
    exc_recv,
):
    me_t = lax.axis_index("trip")
    me_e = lax.axis_index("exc")
    barrier = pltpu.get_barrier_semaphore()
    for step in range(1, n_exc):
        peer = lax.rem(me_e + step, n_exc)
        pl.semaphore_signal(barrier, inc=1, device_id={"exc": peer}, device_id_type=MESH)
    for step in range(1, n_trip):
        peer = lax.rem(me_t + step, n_trip)
        pl.semaphore_signal(barrier, inc=1, device_id={"trip": peer}, device_id_type=MESH)
    lane = lax.broadcasted_iota(jnp.int32, (1, LANES), 1)
    for column in range(n_exc):
        wanted = routing_ref[0, column, 0]
        send_grid[column] = grids_ref[wanted]
        send_mode[column] = jnp.where(
            lane == 0,
            modes_ref[wanted, 0],
            jnp.where(lane == 1, modes_ref[wanted, 1], modes_ref[wanted, 2]),
        )
    table_ref[me_t] = modals_ref[...]
    levels_ref[me_t] = energies_ref[...]
    grid_out_ref[me_e] = send_grid[me_e]
    mode_out_ref[me_e] = send_mode[me_e]
    pl.semaphore_wait(barrier, n_exc - 1 + n_trip - 1)

    def trip_copies(step, slot):
        peer = lax.rem(me_t + step, n_trip)
        for kind, (src, dst) in enumerate(((modals_ref, table_ref), (energies_ref, levels_ref))):
            yield pltpu.make_async_remote_copy(
                src_ref=src,
                dst_ref=dst.at[slot],
                send_sem=trip_send.at[kind, step],
                recv_sem=trip_recv.at[kind, step],
                device_id={"trip": peer},
                device_id_type=MESH,
            )

    def exc_copies(step, slot):
        peer = lax.rem(me_e + step, n_exc)
        for kind, (src, dst) in enumerate(((send_grid, grid_out_ref), (send_mode, mode_out_ref))):
            yield pltpu.make_async_remote_copy(
                src_ref=src.at[peer],
                dst_ref=dst.at[slot],
                send_sem=exc_send.at[kind, step],
                recv_sem=exc_recv.at[kind, step],
                device_id={"exc": peer},
                device_id_type=MESH,
            )

    for step in range(1, n_exc):
        for copy in exc_copies(step, me_e):
            copy.start()
    for step in range(1, n_trip):
        for copy in trip_copies(step, me_t):
            copy.start()
    for step in range(1, n_trip):
        for copy in trip_copies(step, lax.rem(me_t + n_trip - step, n_trip)):
            copy.wait_recv()
    for step in range(1, n_exc):
        for copy in exc_copies(step, lax.rem(me_e + n_exc - step, n_exc)):
            copy.wait_recv()
    for step in range(1, n_trip):
        for copy in trip_copies(step, me_t):
            copy.wait_send()
    for step in range(1, n_exc):
        for copy in exc_copies(step, me_e):
            copy.wait_send()


def iota(shape, axis):
    return lax.broadcasted_iota(jnp.int32, shape, axis)


def spread_by(entries, picker):
    high = entries.astype(BF16)
    rest = entries - high.astype(F32)
    mid = rest.astype(BF16)
    low = (rest - mid.astype(F32)).astype(BF16)
    dot = functools.partial(jnp.dot, preferred_element_type=F32)
    return (dot(high, picker) + dot(mid, picker)) + dot(low, picker)


PAIRS = [(a, a2) for a in range(NMOD) for a2 in range(a, NMOD)]
SLOT = {pair: index for index, pair in enumerate(PAIRS)}


def sigma_kernel(
    n_exc,
    n_blk,
    modes_ref,
    source_ref,
    live_ref,
    table_ref,
    levels_ref,
    grid_ref,
    spec_ref,
    vec_hbm,
    out_hbm,
    vec,
    out,
    mats,
    u_ref,
    left_high,
    left_low,
    picks,
    result,
    spread_ref,
    in_sem,
    out_sem,
):
    per = table_ref.shape[1]
    states = vec.shape[1]
    width = vec.shape[2]
    rows = spec_ref.shape[1]
    sub = NMOD * NMOD
    gg = G * G

    def fetch(b):
        return pltpu.make_async_copy(vec_hbm.at[b], vec.at[b], in_sem.at[b])

    def put(b):
        return pltpu.make_async_copy(out.at[b], out_hbm.at[b], out_sem.at[b])

    @pl.loop(0, n_blk)
    def _(b):
        fetch(b).start()

    key = iota((NMOD * G, gg), 0) % G
    col = iota((NMOD * G, gg), 1)
    picks[0] = jnp.where(key == col // G, 1.0, 0.0).astype(BF16)
    picks[1] = jnp.where(key == col % G, 1.0, 0.0).astype(BF16)
    per_row = width // rows
    row_pick = jnp.where(
        iota((rows, width), 0) == iota((rows, width), 1) // per_row, 1.0, 0.0
    ).astype(BF16)
    spread_ref[...] = spread_by(spec_ref[...], row_pick)[:, None, :]

    owner = iota((sub, NMOD * G), 1) // G
    row = iota((sub, NMOD * G), 0)
    is_first = owner == row // NMOD
    is_second = owner == row % NMOD
    lane = iota((sub, LANES), 1)
    lane_row = iota((sub, LANES), 0)
    lane8 = iota((sub, NMOD), 1)
    row8 = iota((sub, NMOD), 0)

    @pl.loop(0, n_exc)
    def _(p):
        def table_row(which):
            m = modes_ref[p, 0, which]
            return (
                table_ref[m // per, pl.ds(m % per, 1), :],
                levels_ref[m // per, pl.ds(m % per, 1), :],
            )

        phi_i, e_i = table_row(0)
        phi_j, e_j = table_row(1)
        phi_k, e_k = table_row(2)
        tall_j = spread_by(jnp.where(is_first, phi_j, 0.0), picks[0])
        tall_k = spread_by(jnp.where(is_second, phi_k, 0.0), picks[1])
        phi = tall_j * tall_k
        pick_i = picks[1, :, :LANES]
        pair_i = spread_by(jnp.where(is_first, phi_i, 0.0), pick_i) * spread_by(
            jnp.where(is_second, phi_i, 0.0), pick_i
        )
        u_ref[...] = jnp.dot(
            pair_i[:, :G],
            grid_ref[p],
            preferred_element_type=F32,
            precision=lax.Precision.HIGHEST,
        )
        for index, (a, a2) in enumerate(PAIRS):
            line = a * NMOD + a2
            full = phi * u_ref[line : line + 1, :]
            high = full.astype(BF16)
            left_high[index * sub : (index + 1) * sub, :] = high
            left_low[index * sub : (index + 1) * sub, :] = (full - high.astype(F32)).astype(BF16)
        phi_high = phi.astype(BF16)
        phi_low = (phi - phi_high.astype(F32)).astype(BF16)
        right = jnp.concatenate([phi_high, phi_high, phi_low, phi_low], axis=0)
        over = (((1,), (1,)), ((), ()))
        both = lax.dot_general(left_high[...], right, over, preferred_element_type=F32)
        rest = lax.dot_general(
            left_low[...], right[: 2 * sub], over, preferred_element_type=F32
        )
        result[...] = both[:, :LANES] + (both[:, LANES:] + rest)
        e_bc = jnp.sum(
            jnp.where(lane8 == row8 // NMOD, e_j, 0.0) + jnp.where(lane8 == row8 % NMOD, e_k, 0.0),
            axis=1,
            keepdims=True,
        )
        for a in range(NMOD):
            for half in range(NMOD // 2):
                even = SLOT[tuple(sorted((a, 2 * half)))]
                odd = SLOT[tuple(sorted((a, 2 * half + 1)))]
                tile = jnp.where(
                    lane < sub,
                    result[even * sub : (even + 1) * sub, :],
                    result[odd * sub : (odd + 1) * sub, :],
                )
                if a // 2 == half:
                    diagonal = e_bc + e_i[:, a : a + 1]
                    tile = tile + jnp.where(lane == lane_row + (a % 2) * sub, diagonal, 0.0)
                mats[p, a * sub : (a + 1) * sub, half * LANES : (half + 1) * LANES] = tile.astype(
                    BF16
                )

    half_width = width // 2
    half_rows = rows // 2

    @pl.loop(0, n_blk)
    def _(b):
        fetch(b).wait()
        source = source_ref[b]
        live = live_ref[b]

        def part(first):
            cols = slice(first, first + half_width)
            coeff = vec[b, :, cols]
            product = jnp.dot(mats[source], coeff, preferred_element_type=F32)
            summed = product + spread_ref[b, :, cols] * coeff.astype(F32)
            owner_row = (iota((1, half_width), 1) + first) // per_row
            out[b, :, cols] = jnp.where(owner_row < live, summed, 0.0).astype(BF16)

        part(0)

        @pl.when(live > half_rows)
        def _():
            part(half_width)

        @pl.when(live <= half_rows)
        def _():
            out[b, :, half_width:] = jnp.zeros((states, half_width), BF16)

        put(b).start()

    @pl.loop(0, n_blk)
    def _(b):
        put(b).wait()


def solution(mesh):
    n_trip, n_exc = mesh.shape["trip"], mesh.shape["exc"]
    vmem = pl.BlockSpec(memory_space=pltpu.VMEM)
    smem = pl.BlockSpec(memory_space=pltpu.SMEM)
    anywhere = pl.BlockSpec(memory_space=pl.ANY)

    def on_device(
        pes_grids,
        modals,
        energies,
        triple_modes,
        routing,
        block_source,
        live_rows,
        trial_vectors,
        spectator_energy,
    ):
        n_blk, states, width = trial_vectors.shape
        grid_shape = pes_grids.shape[1:]
        table, levels, grids, modes = pl.pallas_call(
            functools.partial(exchange, n_trip, n_exc),
            out_shape=(
                jax.ShapeDtypeStruct((n_trip,) + modals.shape, F32),
                jax.ShapeDtypeStruct((n_trip,) + energies.shape, F32),
                jax.ShapeDtypeStruct((n_exc,) + grid_shape, F32),
                jax.ShapeDtypeStruct((n_exc, 1, LANES), jnp.int32),
            ),
            in_specs=[smem, smem, vmem, vmem, vmem],
            out_specs=(vmem, vmem, vmem, vmem),
            scratch_shapes=[
                pltpu.VMEM((n_exc,) + grid_shape, F32),
                pltpu.VMEM((n_exc, 1, LANES), jnp.int32),
                pltpu.SemaphoreType.DMA((2, n_trip)),
                pltpu.SemaphoreType.DMA((2, n_trip)),
                pltpu.SemaphoreType.DMA((2, n_exc)),
                pltpu.SemaphoreType.DMA((2, n_exc)),
            ],
            compiler_params=pltpu.CompilerParams(collective_id=0, has_side_effects=True),
            name="exchange",
        )(routing, triple_modes, pes_grids, modals, energies)
        sub = NMOD * NMOD
        return pl.pallas_call(
            functools.partial(sigma_kernel, n_exc, n_blk),
            out_shape=jax.ShapeDtypeStruct(trial_vectors.shape, BF16),
            in_specs=[smem, smem, smem, vmem, vmem, vmem, vmem, anywhere],
            out_specs=anywhere,
            scratch_shapes=[
                pltpu.VMEM((n_blk, states, width), BF16),
                pltpu.VMEM((n_blk, states, width), BF16),
                pltpu.VMEM((n_exc, states, states), BF16),
                pltpu.VMEM((sub, G * G), F32),
                pltpu.VMEM((len(PAIRS) * sub, G * G), BF16),
                pltpu.VMEM((len(PAIRS) * sub, G * G), BF16),
                pltpu.VMEM((2, NMOD * G, G * G), BF16),
                pltpu.VMEM((len(PAIRS) * sub, LANES), F32),
                pltpu.VMEM((n_blk, 1, width), F32),
                pltpu.SemaphoreType.DMA((n_blk,)),
                pltpu.SemaphoreType.DMA((n_blk,)),
            ],
            compiler_params=pltpu.CompilerParams(vmem_limit_bytes=60 * 1024 * 1024),
            name="sigma",
        )(modes, block_source, live_rows, table, levels, grids, spectator_energy, trial_vectors)

    in_specs = (
        P(("trip", "exc"), None, None),
        P("trip", None),
        P("trip", None),
        P(("trip", "exc"), None),
        P("trip", None, "exc"),
        P(("trip", "exc")),
        P(("trip", "exc")),
        P(("trip", "exc"), None, None),
        P(("trip", "exc"), None),
    )
    return jax.shard_map(
        on_device,
        mesh=mesh,
        in_specs=in_specs,
        out_specs=P(("trip", "exc"), None, None),
        check_vma=False,
    )
```

time: 554 us -> 40.7 us (0.07)
  matrix products: 213 us -> 0 us
  local copies, waits for them, and re-layouts: 157 us -> 4.05 us
  waiting for transfers between devices: 93.7 us -> 0 us
  loops' own time: 44.5 us -> 0 us
  Pallas kernels: 0 us -> 36.6 us
  other arithmetic: 25.1 us -> 0 us
  blocking collectives: 12.2 us -> 0 us
  starting transfers between devices: 6.19 us -> 0 us
    dot_general x38 -> x0, matrix products: 213 us -> none  [the longest x4 146 us: integrals(): jnp.einsum('xbc,ax->abc', section_two, paired[0], precision=lax.Precision...]
    all_to_all x1 -> x0, waiting for transfers between devices: 93.7 us -> none  [on_device(): lax.all_to_all(jnp.take(owned, targets, axis=0), 'exc', split_axis=0, con...]
    transpose x4 -> x0, local copies, waits for them, and re-layouts: 60.9 us -> none  [integrals(): matrix = tensor.reshape(NMOD, NMOD, NMOD, NMOD, NMOD, NMOD).transpose(0,...]
    reshape x10 -> x0, local copies, waits for them, and re-layouts: 50.8 us -> none  [the longest x4 50.4 us: integrals(): matrix = tensor.reshape(NMOD, NMOD, NMOD, NMOD, NMOD, NMOD).transpose(0,...]
    another operation x2 -> x0, loops' own time: 44.5 us -> none  [the longest x1 44.2 us: on_device(): lax.map(one_block, (block_source, trial_vectors, spectator_energy, live_r...]
    pallas_call x0 -> x2, Pallas kernels: none -> 36.6 us  [the longest x1 24.8 us: on_device(): pl.pallas_call(functools.partial(sigma_kernel, n_exc, n_blk), out_shape=j...]
    dynamic_slice x60 -> x0, local copies, waits for them, and re-layouts: 32.4 us -> none  [the longest x48 29.4 us: on_device(): lax.map(one_block, (block_source, trial_vectors, spectator_energy, live_r...]
    lt x24 -> x0, other arithmetic: 14.7 us -> none  [apply_block(): column_rows < live_count]
  transfers between devices with their start and end apart: 1 -> 0, of which waited for: 1 -> 0; matrix products, arithmetic and copies ran while one was open for 0% -> 0% of each run, Pallas kernels for 0% -> 0%
where the time goes in v1:
time: 40.7 us; the launch traced here: 40.6 us
  Pallas kernels  36.6 us (90%)
  local copies, waits for them, and re-layouts  4.05 us (10%)
    pallas_call x1, Pallas kernels, on_device(): pl.pallas_call(functools.partial(sigma_kernel, n_exc, n_blk), out_shape=j...  24.8 us
    pallas_call x1, Pallas kernels, on_device(): pl.pallas_call(functools.partial(exchange, n_trip, n_exc), out_shape=(jax...  11.8 us
    unnamed x3, local copies, waits for them, and re-layouts  4.05 us

profile of v1, /device:TPU:0, one launch (start us, length us, event | category | flops | bytes accessed | tf_op | source)
XLA Modules:
  0.0 40.6 jit_solution(12882815830487442893)
XLA Ops:
  0.0 1.3 %copy.10.routing_ref = s32[1,8,1]{2,1,0:T(8,128)} copy(s32[1,8,1]{1,2,0:T(1,128)} %param.13) | data formatting | bytes 64 | tf_op args[4]
  1.3 1.4 %copy.12.spec_ref = f32[24,8]{1,0:T(8,128)} copy(f32[24,8]{0,1:T(8,128)} %param.17) | data formatting | bytes 1536 | tf_op args[8]
  2.7 1.4 %copy.11.energies_ref = f32[50,8]{1,0:T(8,128)} copy(f32[50,8]{0,1:T(8,128)} %param.11) | data formatting | bytes 3200 | tf_op args[2]
  4.0 11.8 %exchange.1 = (f32[4,50,128]{2,1,0:T(8,128)}, f32[4,50,8]{2,1,0:T(8,128)}, f32[8,16,256]{2,1,0:T(8,128)}, s32[8,1,128]{2,1,0:T(1,128)}) custom-call(s32[1,8,1]{2,1,0:T(8,128)} %copy.10.routing_ref, s32[4,3]{1,0:T(4,128)} %modes_ref.1, f32[4,16,256]{2,1,0:T(8,128)} %grids_ref.1, f32[50,128]{1,0:T(8,128)} %modals_ref.1, f32[50,8]{1,0:T(8,128)} %copy.11.energies_ref), custom_call_target="tpu_custom_call" | custom-call | tf_op jit(solution)/shard_map/exchange/pallas_call | solution.py:296
  15.9 24.8 %sigma.1 = bf16[24,512,512]{2,1,0:T(8,128)(2,1)} custom-call(s32[8,1,128]{2,1,0:T(1,128)} %get-tuple-element.9.modes_ref, s32[24]{0:T(128)} %source_ref.1, s32[24]{0:T(128)} %live_ref.1, f32[4,50,128]{2,1,0:T(8,128)} %get-tuple-element.10.table_ref, f32[4,50,8]{2,1,0:T(8,128)} %get-tuple-element.11.levels_ref, f32[8,16,256]{2,1,0:T(8,128)} %get-tuple-element.12.grid_ref, ...), custom_call_target="tpu_custom_call" | custom-call | tf_op jit(solution)/shard_map/sigma/pallas_call | solution.py:318

commit v2 on v1

--- a/solution.py
+++ b/solution.py
@@ -45,7 +45,7 @@
         pl.semaphore_signal(barrier, inc=1, device_id={"trip": peer}, device_id_type=MESH)
     lane = lax.broadcasted_iota(jnp.int32, (1, LANES), 1)
     for column in range(n_exc):
-        wanted = routing_ref[0, column, 0]
+        wanted = routing_ref[0, 0, column]
         send_grid[column] = grids_ref[wanted]
         send_mode[column] = jnp.where(
             lane == 0,
@@ -146,7 +146,7 @@
     per = table_ref.shape[1]
     states = vec.shape[1]
     width = vec.shape[2]
-    rows = spec_ref.shape[1]
+    rows = spec_ref.shape[0]
     sub = NMOD * NMOD
     gg = G * G
 
@@ -168,7 +168,7 @@
     row_pick = jnp.where(
         iota((rows, width), 0) == iota((rows, width), 1) // per_row, 1.0, 0.0
     ).astype(BF16)
-    spread_ref[...] = spread_by(spec_ref[...], row_pick)[:, None, :]
+    spread_ref[...] = spread_by(spec_ref[...].T, row_pick)[:, None, :]
 
     owner = iota((sub, NMOD * G), 1) // G
     row = iota((sub, NMOD * G), 0)
@@ -176,16 +176,16 @@
     is_second = owner == row % NMOD
     lane = iota((sub, LANES), 1)
     lane_row = iota((sub, LANES), 0)
-    lane8 = iota((sub, NMOD), 1)
-    row8 = iota((sub, NMOD), 0)
 
     @pl.loop(0, n_exc)
     def _(p):
         def table_row(which):
             m = modes_ref[p, 0, which]
+            tile = levels_ref[m // per]
+            here = iota(tile.shape, 1) == m % per
             return (
                 table_ref[m // per, pl.ds(m % per, 1), :],
-                levels_ref[m // per, pl.ds(m % per, 1), :],
+                jnp.sum(jnp.where(here, tile, 0.0), axis=1, keepdims=True),
             )
 
         phi_i, e_i = table_row(0)
@@ -219,11 +219,7 @@
             left_low[...], right[: 2 * sub], over, preferred_element_type=F32
         )
         result[...] = both[:, :LANES] + (both[:, LANES:] + rest)
-        e_bc = jnp.sum(
-            jnp.where(lane8 == row8 // NMOD, e_j, 0.0) + jnp.where(lane8 == row8 % NMOD, e_k, 0.0),
-            axis=1,
-            keepdims=True,
-        )
+        e_bc = jnp.concatenate([e_j[b : b + 1, :] + e_k for b in range(NMOD)], axis=0)
         for a in range(NMOD):
             for half in range(NMOD // 2):
                 even = SLOT[tuple(sorted((a, 2 * half)))]
@@ -234,7 +230,7 @@
                     result[odd * sub : (odd + 1) * sub, :],
                 )
                 if a // 2 == half:
-                    diagonal = e_bc + e_i[:, a : a + 1]
+                    diagonal = e_bc + e_i[a : a + 1, :]
                     tile = tile + jnp.where(lane == lane_row + (a % 2) * sub, diagonal, 0.0)
                 mats[p, a * sub : (a + 1) * sub, half * LANES : (half + 1) * LANES] = tile.astype(
                     BF16
@@ -297,7 +293,7 @@
             functools.partial(exchange, n_trip, n_exc),
             out_shape=(
                 jax.ShapeDtypeStruct((n_trip,) + modals.shape, F32),
-                jax.ShapeDtypeStruct((n_trip,) + energies.shape, F32),
+                jax.ShapeDtypeStruct((n_trip,) + energies.T.shape, F32),
                 jax.ShapeDtypeStruct((n_exc,) + grid_shape, F32),
                 jax.ShapeDtypeStruct((n_exc, 1, LANES), jnp.int32),
             ),
@@ -313,7 +309,7 @@
             ],
             compiler_params=pltpu.CompilerParams(collective_id=0, has_side_effects=True),
             name="exchange",
-        )(routing, triple_modes, pes_grids, modals, energies)
+        )(jnp.swapaxes(routing, 1, 2), triple_modes, pes_grids, modals, energies.T)
         sub = NMOD * NMOD
         return pl.pallas_call(
             functools.partial(sigma_kernel, n_exc, n_blk),
@@ -335,7 +331,7 @@
             ],
             compiler_params=pltpu.CompilerParams(vmem_limit_bytes=60 * 1024 * 1024),
             name="sigma",
-        )(modes, block_source, live_rows, table, levels, grids, spectator_energy, trial_vectors)
+        )(modes, block_source, live_rows, table, levels, grids, spectator_energy.T, trial_vectors)
 
     in_specs = (
         P(("trip", "exc"), None, None),

time: 40.7 us -> 35.2 us (0.86)
  the two profiles are of different devices: /device:TPU:0 before, /device:TPU:1 now
where the time goes in v2:
time: 35.2 us; the launch traced here: 34.6 us
  Pallas kernels  34.6 us (98%)
    pallas_call x1, Pallas kernels, on_device(): pl.pallas_call(functools.partial(sigma_kernel, n_exc, n_blk), out_shape=j...  23.4 us
    pallas_call x1, Pallas kernels, on_device(): pl.pallas_call(functools.partial(exchange, n_trip, n_exc), out_shape=(jax...  11.2 us

profile of v2, /device:TPU:1, one launch (start us, length us, event | category | flops | bytes accessed | tf_op | source)
XLA Modules:
  0.0 34.6 jit_solution(11449941042904993795)
XLA Ops:
  0.0 11.2 %exchange.1 = (f32[4,50,128]{2,1,0:T(8,128)}, f32[4,8,50]{2,1,0:T(8,128)}, f32[8,16,256]{2,1,0:T(8,128)}, s32[8,1,128]{2,1,0:T(1,128)}) custom-call(s32[1,1,8]{2,1,0:T(1,128)} %bitcast.5, s32[4,3]{1,0:T(4,128)} %modes_ref.1, f32[4,16,256]{2,1,0:T(8,128)} %grids_ref.1, f32[50,128]{1,0:T(8,128)} %modals_ref.1, f32[8,50]{1,0:T(8,128)} %bitcast.4), custom_call_target="tpu_custom_call" | custom-call | tf_op jit(solution)/shard_map/exchange/pallas_call | solution.py:292
  11.2 23.4 %sigma.1 = bf16[24,512,512]{2,1,0:T(8,128)(2,1)} custom-call(s32[8,1,128]{2,1,0:T(1,128)} %get-tuple-element.9.modes_ref, s32[24]{0:T(128)} %source_ref.1, s32[24]{0:T(128)} %live_ref.1, f32[4,50,128]{2,1,0:T(8,128)} %get-tuple-element.10.table_ref, f32[4,8,50]{2,1,0:T(8,128)} %get-tuple-element.11.levels_ref, f32[8,16,256]{2,1,0:T(8,128)} %get-tuple-element.12.grid_ref, ...), custom_call_target="tpu_custom_call" | custom-call | tf_op jit(solution)/shard_map/sigma/pallas_call | solution.py:314
